TPU v7x, 512 devices: a whole 4x4x16 slice. The times are simulated.
512 devices in a mesh: head: 16 (over z), span: 32 (over x, y, core).
Axes of the slice: x: 4, y: 4, z: 16, core: 2. Of those that a mesh axis runs over, the one named last changes fastest.
Arguments:
- queries: bfloat16 [65536, 2048], P(('span', 'head')), may hold values from -6 to 6
- keys: bfloat16 [65536, 2048], P(('span', 'head')), may hold values from -6 to 6
- values: bfloat16 [65536, 2048], P(('span', 'head')), may hold values from -6 to 6
- out_grad: bfloat16 [65536, 2048], P(('span', 'head')), may hold values from -6 to 6
Outputs:
- attn_out: bfloat16 [65536, 2048], P(('span', 'head'))
- query_gradient: bfloat16 [65536, 2048], P(('span', 'head'))
- grad_key: bfloat16 [65536, 2048], P(('span', 'head'))
- grad_value: bfloat16 [65536, 2048], P(('span', 'head'))
All inputs are finite; a program needn't handle non-finite values.
Results may differ from a plain program's by a relative error of at most 0.0058.
Values may be sent and summed in bfloat16 or wider, within the bound.
A program may use at most 64 MiB of HBM per device.

v0:
```python
import jax
import jax.numpy as jnp
from jax import lax
from jax.sharding import Mesh
from jax.sharding import PartitionSpec as P

HEADS = 16
DH = 128
SPAN = ("span_0", "span_1", "span_2")
SPAN_HEAD = ("span_0", "span_1", "span_2", "head")


def neutral_like(array, identity):
    return jax.tree.map(
        lambda part, zero: jnp.zeros_like(part) + jnp.asarray(zero, part.dtype), array, identity
    )


def prefix_by_axis(array, axes, combine, identity):
    before = start = neutral_like(array, identity)
    so_far = array
    for axis in reversed(axes):
        devices, position = (lax.axis_size(axis), lax.axis_index(axis))
        pieces = jax.tree.map(lambda part: lax.all_gather(part, axis), so_far)
        inside, so_far = (start, start)
        for k in range(devices):
            passed = k < position
            so_far = combine(so_far, jax.tree.map(lambda part: part[k], pieces))
            inside = jax.tree.map(lambda new, old: jnp.where(passed, new, old), so_far, inside)
        before = combine(inside, before)
    return before


def sent_to_all(array, axis):
    devices = lax.axis_size(axis)
    return lax.all_to_all(
        jnp.broadcast_to(array[None], (devices, *array.shape)), axis, 0, 0, tiled=True
    )


def taken_together(array, axis):
    return sent_to_all(array, axis).sum(axis=0)


def plus_pair(earlier, later):
    return (earlier[0] + later[0], earlier[1] + later[1])


def block_work(queries, keys, values, scaled, position_scale, forward_narrow, back_low):
    length = queries.shape[0]
    head_count = queries.shape[1]
    head_width = queries.shape[2]
    row_count = min(512, length)
    outputs = []
    query_grads = []
    key_acc = jnp.zeros((length, head_count, head_width), jnp.float32)
    value_acc = jnp.zeros((length, head_count, head_width), jnp.float32)
    for block_index in range(length // row_count):
        start_row = block_index * row_count
        end_row = start_row + row_count
        query_lines = queries[start_row:end_row]
        scaled_lines = scaled[start_row:end_row]
        key_cols = keys[:end_row]
        value_cols = values[:end_row]
        row_pos = start_row + lax.iota(jnp.int32, row_count)
        col_pos = lax.iota(jnp.int32, end_row)
        causal = col_pos[None, :] <= row_pos[:, None]
        raw_scores = jnp.einsum(
            "tnd,snd->nts", query_lines, key_cols, preferred_element_type=jnp.float32
        )
        scores = jnp.where(causal[None], raw_scores, 0.0).astype(jnp.bfloat16)
        raw_grads = jnp.einsum(
            "tnd,snd->nts", scaled_lines, value_cols, preferred_element_type=jnp.float32
        )
        score_gradient = jnp.where(causal[None], raw_grads, 0.0).astype(jnp.bfloat16)
        local_out = jnp.einsum(
            "epa,aev->pev", scores, value_cols, preferred_element_type=jnp.float32
        )
        carried_result = jnp.einsum(
            "rwb,wbo->rwo", query_lines, forward_narrow, preferred_element_type=jnp.float32
        )
        row_scale = position_scale[start_row:end_row]
        outputs.append(
            ((local_out + carried_result) * row_scale[:, None, None]).astype(jnp.bfloat16)
        )
        local_query = jnp.einsum(
            "epa,aev->pev", score_gradient, key_cols, preferred_element_type=jnp.float32
        )
        carried_query = jnp.einsum(
            "hsx,smx->hsm", scaled_lines, forward_narrow, preferred_element_type=jnp.float32
        )
        query_grads.append((local_query + carried_query).astype(jnp.bfloat16))
        key_acc = key_acc.at[:end_row].add(
            jnp.einsum(
                "nts,tnd->snd", score_gradient, query_lines, preferred_element_type=jnp.float32
            )
        )
        value_acc = value_acc.at[:end_row].add(
            jnp.einsum("nts,tnd->snd", scores, scaled_lines, preferred_element_type=jnp.float32)
        )
    grad_key = (
        key_acc + jnp.einsum("snv,nvk->snk", values, back_low, preferred_element_type=jnp.float32)
    ).astype(jnp.bfloat16)
    grad_value = (
        value_acc + jnp.einsum("snk,nvk->snv", keys, back_low, preferred_element_type=jnp.float32)
    ).astype(jnp.bfloat16)
    return (
        jnp.concatenate(outputs, axis=0),
        jnp.concatenate(query_grads, axis=0),
        grad_key,
        grad_value,
    )


def attend(pieces):
    queries = pieces[0][:, 0]
    keys = pieces[1][:, 0]
    values = pieces[2][:, 0]
    out_grad = pieces[3][:, 0]
    length = queries.shape[0]
    head_width = queries.shape[2]
    span_index = lax.axis_index(SPAN)
    position = span_index * length + lax.iota(jnp.int32, length)
    position_scale = 1.0 / jnp.sqrt(jnp.float32(head_width) * (position + 1).astype(jnp.float32))
    scaled = (out_grad.astype(jnp.float32) * position_scale[:, None, None]).astype(jnp.bfloat16)
    forward_within = jnp.einsum("xgy,xgi->gyi", keys, values, preferred_element_type=jnp.float32)
    back_local = jnp.einsum("tnv,tnk->nvk", scaled, queries, preferred_element_type=jnp.float32)
    zeros_state = jnp.zeros_like(forward_within)
    fwd_state, back_below = prefix_by_axis(
        (forward_within, back_local), SPAN, plus_pair, (zeros_state, zeros_state)
    )
    back_whole = taken_together(back_local, SPAN)
    back_state = back_whole - back_below - back_local
    forward_narrow = fwd_state.astype(jnp.bfloat16)
    back_low = back_state.astype(jnp.bfloat16)
    results = block_work(queries, keys, values, scaled, position_scale, forward_narrow, back_low)
    return (results[0][:, None], results[1][:, None], results[2][:, None], results[3][:, None])


def split_heads(matrix, group_count):
    return matrix.reshape(matrix.shape[0], group_count, HEADS // group_count, DH)


def merge_heads(grouped):
    return grouped.reshape(grouped.shape[0], HEADS * DH)


def shards(queries, keys, values, out_grad):
    group_count = lax.axis_size("head")
    results = attend(
        (
            lax.all_to_all(
                split_heads(queries, group_count), "head", split_axis=1, concat_axis=0, tiled=True
            ),
            lax.all_to_all(
                split_heads(keys, group_count), "head", split_axis=1, concat_axis=0, tiled=True
            ),
            lax.all_to_all(
                split_heads(values, group_count), "head", split_axis=1, concat_axis=0, tiled=True
            ),
            lax.all_to_all(
                split_heads(out_grad, group_count), "head", split_axis=1, concat_axis=0, tiled=True
            ),
        )
    )
    returned = (
        lax.all_to_all(results[0], "head", split_axis=0, concat_axis=1, tiled=True),
        lax.all_to_all(results[1], "head", split_axis=0, concat_axis=1, tiled=True),
        lax.all_to_all(results[2], "head", split_axis=0, concat_axis=1, tiled=True),
        lax.all_to_all(results[3], "head", split_axis=0, concat_axis=1, tiled=True),
    )
    return (
        merge_heads(returned[0]),
        merge_heads(returned[1]),
        merge_heads(returned[2]),
        merge_heads(returned[3]),
    )


def solution(mesh):
    finer = Mesh(
        mesh.devices.reshape(mesh.shape["head"], 4, 4, 2), ("head", "span_0", "span_1", "span_2")
    )
    placed = (P(SPAN_HEAD, None), P(SPAN_HEAD, None), P(SPAN_HEAD, None), P(SPAN_HEAD, None))
    return jax.shard_map(
        shards,
        mesh=finer,
        in_specs=placed,
        out_specs=(P(SPAN_HEAD, None), P(SPAN_HEAD, None), P(SPAN_HEAD, None), P(SPAN_HEAD, None)),
        check_vma=False,
    )
```

profile of v0, /device:TPU:64, one launch (start us, length us, event | category | flops | bytes accessed | tf_op | source)
XLA Modules:
  0.0 339.3 jit_solution(2096342704361226328)
XLA Ops:
  0.6 2.1 copy.164
  2.7 14.9 %all-to-all-start.1 = ((bf16[128,16,1,128]{0,3,2,1:T(8,128)(2,1)}), bf16[128,16,1,128]{0,3,2,1:T(8,128)(2,1)S(1)}, u32[]{:S(2)}, u32[]{:S(2)}) async-start(bf16[128,16,1,128]{0,3,2,1:T(8,128)(2,1)} %bitcast.5), calls=%async_computation.1 | async-start | bytes 1048576 | tf_op jit(solution)/shard_map/all_to_all | solution.py:155
  17.9 1.0 copy.167
  18.9 26.1 %all-to-all-done.1 = bf16[128,16,1,128]{0,3,2,1:T(8,128)(2,1)S(1)} async-done(((bf16[128,16,1,128]{0,3,2,1:T(8,128)(2,1)}), bf16[128,16,1,128]{0,3,2,1:T(8,128)(2,1)S(1)}, u32[]{:S(2)}, u32[]{:S(2)}) %all-to-all-start.1) | async-done | bytes 524320 | tf_op jit(solution)/shard_map/all_to_all | solution.py:155
  45.0 8.0 %all-to-all-start.2 = ((bf16[128,16,1,128]{3,0,2,1:T(8,128)(2,1)}), bf16[128,16,1,128]{3,0,2,1:T(8,128)(2,1)S(1)}, u32[]{:S(2)}, u32[]{:S(2)}) async-start(bf16[128,16,1,128]{3,0,2,1:T(8,128)(2,1)} %copy.167), calls=%async_computation.2 | async-start | bytes 1048576 | tf_op jit(solution)/shard_map/all_to_all | solution.py:158
  53.0 1.0 copy.161
  54.0 26.4 %all-to-all-done.2 = bf16[128,16,1,128]{3,0,2,1:T(8,128)(2,1)S(1)} async-done(((bf16[128,16,1,128]{3,0,2,1:T(8,128)(2,1)}), bf16[128,16,1,128]{3,0,2,1:T(8,128)(2,1)S(1)}, u32[]{:S(2)}, u32[]{:S(2)}) %all-to-all-start.2) | async-done | bytes 524320 | tf_op jit(solution)/shard_map/all_to_all | solution.py:158
  80.4 8.1 %all-to-all-start = ((bf16[128,16,1,128]{0,3,2,1:T(8,128)(2,1)}), bf16[128,16,1,128]{0,3,2,1:T(8,128)(2,1)S(1)}, u32[]{:S(2)}, u32[]{:S(2)}) async-start(bf16[128,16,1,128]{0,3,2,1:T(8,128)(2,1)} %bitcast.1), calls=%async_computation | async-start | bytes 1048576 | tf_op jit(solution)/shard_map/all_to_all | solution.py:152
  88.4 1.0 copy.177
  89.6 0.7 slice.370
  90.4 0.9 copy.169
  91.6 1.9 all-gather
  93.5 12.8 %all-gather.2 = f32[512,128]{1,0:T(8,128)S(1)} all-gather(f32[128,128]{1,0:T(8,128)S(1)} %slice_add_fusion.13), channel_id=4, replica_groups=mesh['head'=16,'span_0'=4,'span_1'=4,'span_2'=2] {'span_1'}, dimensions={0}, use_global_device_ids=true | all-gather | bytes 327680 | tf_op jit(solution)/shard_map/all_gather | solution.py:24
  106.3 13.5 %all_gather.29 = f32[4,1,128,128]{3,2,1,0:T(8,128)} all-gather(f32[1,1,128,128]{3,2,1,0:T(8,128)S(1)} %fusion.61), channel_id=1, replica_groups=mesh['head'=16,'span_0'=4,'span_1'=4,'span_2'=2] {'span_0'}, dimensions={0}, use_global_device_ids=true | all-gather | bytes 327680 | tf_op jit(solution)/shard_map/all_gather | solution.py:24
  119.8 12.2 %all-to-all-start.4 = ((bf16[128,16,1,128]{0,3,2,1:T(8,128)(2,1)}), bf16[128,16,1,128]{0,3,2,1:T(8,128)(2,1)}, u32[]{:S(2)}, u32[]{:S(2)}) async-start(bf16[128,16,1,128]{0,3,2,1:T(8,128)(2,1)} %bitcast.48), calls=%async_computation.4 | async-start | bytes 1048576 | tf_op jit(solution)/shard_map/all_to_all | solution.py:161
  134.6 0.8 fusion.40
  135.4 0.8 fusion.41
  136.2 0.8 slice.373
  137.3 0.8 slice.374
  138.2 2.0 copy.171
  140.1 1.6 fusion
  143.3 1.3 copy-done
  146.1 1.6 reduce.17
  147.8 2.0 reshape.1005
  149.7 6.5 %all-to-all-done.4 = bf16[128,16,1,128]{0,3,2,1:T(8,128)(2,1)} async-done(((bf16[128,16,1,128]{0,3,2,1:T(8,128)(2,1)}), bf16[128,16,1,128]{0,3,2,1:T(8,128)(2,1)}, u32[]{:S(2)}, u32[]{:S(2)}) %all-to-all-start.4) | async-done | bytes 524320 | tf_op jit(solution)/shard_map/all_to_all | solution.py:161
  156.2 6.6 %all-to-all-start.3 = ((bf16[16,2,8192]{2,1,0:T(2,128)(2,1)}), bf16[16,2,8192]{2,1,0:T(2,128)(2,1)}, u32[]{:S(2)}, u32[]{:S(2)}) async-start(bf16[16,2,8192]{2,1,0:T(2,128)(2,1)} %reshape.1005), calls=%async_computation.3 | async-start | bytes 1048576 | tf_op jit(solution)/shard_map/all_to_all | solution.py:167
  162.8 1.3 copy.179
  165.0 0.8 copy-done.14
  166.5 1.0 copy-done.12
  167.5 1.1 convolution_bitcast_fusion.14
  169.4 19.9 %all-to-all-done.3 = bf16[16,2,8192]{2,1,0:T(2,128)(2,1)} async-done(((bf16[16,2,8192]{2,1,0:T(2,128)(2,1)}), bf16[16,2,8192]{2,1,0:T(2,128)(2,1)}, u32[]{:S(2)}, u32[]{:S(2)}) %all-to-all-start.3) | async-done | bytes 524320 | tf_op jit(solution)/shard_map/all_to_all | solution.py:167
  189.2 1.6 broadcast_in_dim.71
  190.9 8.1 %all-to-all-start.6 = ((f32[32,1,128,128]{3,2,1,0:T(8,128)}), f32[32,1,128,128]{3,2,1,0:T(8,128)}, u32[]{:S(2)}, u32[]{:S(2)}) async-start(f32[32,1,128,128]{3,2,1,0:T(8,128)} %broadcast_in_dim.71), calls=%async_computation.6 | async-start | bytes 4194304 | tf_op jit(solution)/shard_map/all_to_all | solution.py:36
  199.1 1.1 fusion.38
  200.3 1.6 fusion.1
  204.0 1.3 copy-done.2
  206.2 0.8 maximum_bitcast_fusion.1
  207.0 2.7 reduce.18
  209.7 2.0 reshape.1007
  212.1 1.9 all-gather.1
  214.0 13.7 %all-to-all-done.6 = f32[32,1,128,128]{3,2,1,0:T(8,128)} async-done(((f32[32,1,128,128]{3,2,1,0:T(8,128)}), f32[32,1,128,128]{3,2,1,0:T(8,128)}, u32[]{:S(2)}, u32[]{:S(2)}) %all-to-all-start.6) | async-done | bytes 2097184 | tf_op jit(solution)/shard_map/all_to_all | solution.py:36
  227.7 6.5 %all-to-all-start.5 = ((bf16[16,2,8192]{2,1,0:T(2,128)(2,1)}), bf16[16,2,8192]{2,1,0:T(2,128)(2,1)}, u32[]{:S(2)}, u32[]{:S(2)}) async-start(bf16[16,2,8192]{2,1,0:T(2,128)(2,1)} %reshape.1007), calls=%async_computation.5 | async-start | bytes 1048576 | tf_op jit(solution)/shard_map/all_to_all | solution.py:168
  234.1 12.7 %all-gather.3 = f32[512,128]{1,0:T(8,128)S(1)} all-gather(f32[128,128]{1,0:T(8,128)S(1)} %slice_add_fusion.6), channel_id=5, replica_groups=mesh['head'=16,'span_0'=4,'span_1'=4,'span_2'=2] {'span_1'}, dimensions={0}, use_global_device_ids=true | all-gather | bytes 327680 | tf_op jit(solution)/shard_map/all_gather | solution.py:24
  246.9 13.0 %all_gather.32 = f32[4,1,128,128]{3,2,1,0:T(8,128)} all-gather(f32[1,1,128,128]{3,2,1,0:T(8,128)S(1)} %fusion.57), channel_id=1, replica_groups=mesh['head'=16,'span_0'=4,'span_1'=4,'span_2'=2] {'span_0'}, dimensions={0}, use_global_device_ids=true | all-gather | bytes 327680 | tf_op jit(solution)/shard_map/all_gather | solution.py:24
  259.9 1.6 fusion.19
  262.0 1.2 copy-done.1
  263.6 1.8 reduce_sum.9
  265.8 1.0 reduce.20
  267.2 0.9 reshape.1011
  268.1 12.0 %all-to-all-start.8 = ((bf16[16,2,8192]{2,1,0:T(2,128)(2,1)}), bf16[16,2,8192]{2,1,0:T(2,128)(2,1)S(1)}, u32[]{:S(2)}, u32[]{:S(2)}) async-start(bf16[16,2,8192]{2,1,0:T(2,128)(2,1)} %reshape.1011), calls=%async_computation.8 | async-start | bytes 1048576 | tf_op jit(solution)/shard_map/all_to_all | solution.py:170
  281.5 0.7 fusion.3
  282.2 0.9 copy-done.3
  283.1 0.7 fusion.8
  284.1 1.0 reduce.19
  285.1 0.9 reshape.1009
  286.0 17.6 %all-to-all-done.8 = bf16[16,2,8192]{2,1,0:T(2,128)(2,1)S(1)} async-done(((bf16[16,2,8192]{2,1,0:T(2,128)(2,1)}), bf16[16,2,8192]{2,1,0:T(2,128)(2,1)S(1)}, u32[]{:S(2)}, u32[]{:S(2)}) %all-to-all-start.8) | async-done | bytes 524320 | tf_op jit(solution)/shard_map/all_to_all | solution.py:170
  303.7 7.4 %all-to-all-start.7 = ((bf16[16,2,8192]{2,1,0:T(2,128)(2,1)}), bf16[16,2,8192]{2,1,0:T(2,128)(2,1)S(1)}, u32[]{:S(2)}, u32[]{:S(2)}) async-start(bf16[16,2,8192]{2,1,0:T(2,128)(2,1)} %reshape.1009), calls=%async_computation.7 | async-start | bytes 1048576 | tf_op jit(solution)/shard_map/all_to_all | solution.py:169
  311.1 2.2 reshape.1006
  313.7 1.0 copy.191
  314.7 2.2 reshape.1008
  317.3 1.0 copy.192
  319.2 1.0 copy.194
  320.2 17.2 %all-to-all-done.7 = bf16[16,2,8192]{2,1,0:T(2,128)(2,1)S(1)} async-done(((bf16[16,2,8192]{2,1,0:T(2,128)(2,1)}), bf16[16,2,8192]{2,1,0:T(2,128)(2,1)S(1)}, u32[]{:S(2)}, u32[]{:S(2)}) %all-to-all-start.7) | async-done | bytes 524320 | tf_op jit(solution)/shard_map/all_to_all | solution.py:169
  338.3 1.0 copy.193
  (153 shorter events, 17.7 us)
Async XLA Ops:
  0.6 17.0 %copy-start.42 = (bf16[128,2048]{1,0:T(8,128)(2,1)S(1)}, bf16[128,2048]{1,0:T(8,128)(2,1)}, u32[]{:S(2)}) copy-start(bf16[128,2048]{1,0:T(8,128)(2,1)} %param.26) | copy-start | bytes 1572868
  2.7 50.3 %copy-start.43 = (bf16[128,2048]{1,0:T(8,128)(2,1)S(1)}, bf16[128,2048]{1,0:T(8,128)(2,1)}, u32[]{:S(2)}) copy-start(bf16[128,2048]{1,0:T(8,128)(2,1)} %param.24) | copy-start | bytes 1572868
  2.7 42.3 %all-to-all-start.1 = ((bf16[128,16,1,128]{0,3,2,1:T(8,128)(2,1)}), bf16[128,16,1,128]{0,3,2,1:T(8,128)(2,1)S(1)}, u32[]{:S(2)}, u32[]{:S(2)}) async-start(bf16[128,16,1,128]{0,3,2,1:T(8,128)(2,1)} %bitcast.5), calls=%async_computation.1 | async-start | bytes 1048576 | tf_op jit(solution)/shard_map/all_to_all | solution.py:155
  17.9 70.5 %copy-start.44 = (bf16[128,2048]{1,0:T(8,128)(2,1)S(1)}, bf16[128,2048]{1,0:T(8,128)(2,1)}, u32[]{:S(2)}) copy-start(bf16[128,2048]{1,0:T(8,128)(2,1)} %param.27) | copy-start | bytes 1572868
  45.0 35.4 %all-to-all-start.2 = ((bf16[128,16,1,128]{3,0,2,1:T(8,128)(2,1)}), bf16[128,16,1,128]{3,0,2,1:T(8,128)(2,1)S(1)}, u32[]{:S(2)}, u32[]{:S(2)}) async-start(bf16[128,16,1,128]{3,0,2,1:T(8,128)(2,1)} %copy.167), calls=%async_computation.2 | async-start | bytes 1048576 | tf_op jit(solution)/shard_map/all_to_all | solution.py:158
  80.4 39.5 %all-to-all-start = ((bf16[128,16,1,128]{0,3,2,1:T(8,128)(2,1)}), bf16[128,16,1,128]{0,3,2,1:T(8,128)(2,1)S(1)}, u32[]{:S(2)}, u32[]{:S(2)}) async-start(bf16[128,16,1,128]{0,3,2,1:T(8,128)(2,1)} %bitcast.1), calls=%async_computation | async-start | bytes 1048576 | tf_op jit(solution)/shard_map/all_to_all | solution.py:152
  89.5 43.2 %copy-start.38 = (bf16[4,128,1,1,128]{4,1,0,3,2:T(8,128)(2,1)}, bf16[4,128,1,1,128]{4,1,0,3,2:T(8,128)(2,1)S(1)}, u32[]{:S(2)}) copy-start(bf16[4,128,1,1,128]{4,1,0,3,2:T(8,128)(2,1)S(1)} %slice.356) | copy-start | bytes 393220
  90.4 42.0 %copy-start.40 = (bf16[4,128,1,1,128]{4,1,0,3,2:T(8,128)(2,1)}, bf16[4,128,1,1,128]{4,1,0,3,2:T(8,128)(2,1)S(1)}, u32[]{:S(2)}) copy-start(bf16[4,128,1,1,128]{4,1,0,3,2:T(8,128)(2,1)S(1)} %copy.165) | copy-start | bytes 393220
  93.5 12.8 %copy-start.28 = (f32[256,128]{1,0:T(8,128)}, f32[256,128]{1,0:T(8,128)S(1)}, u32[]{:S(2)}) copy-start(f32[256,128]{1,0:T(8,128)S(1)} %all-gather) | copy-start | bytes 393220
  119.8 36.4 %all-to-all-start.4 = ((bf16[128,16,1,128]{0,3,2,1:T(8,128)(2,1)}), bf16[128,16,1,128]{0,3,2,1:T(8,128)(2,1)}, u32[]{:S(2)}, u32[]{:S(2)}) async-start(bf16[128,16,1,128]{0,3,2,1:T(8,128)(2,1)} %bitcast.48), calls=%async_computation.4 | async-start | bytes 1048576 | tf_op jit(solution)/shard_map/all_to_all | solution.py:161
  132.3 1.2 copy-start.36
  132.4 2.2 copy-start.26
  132.4 3.0 copy-start.24
  132.4 9.9 %copy-start.22 = (bf16[4,128,1,1,128]{4,1,0,3,2:T(8,128)(2,1)}, bf16[4,128,1,1,128]{4,1,0,3,2:T(8,128)(2,1)S(1)}, u32[]{:S(2)}) copy-start(bf16[4,128,1,1,128]{4,1,0,3,2:T(8,128)(2,1)S(1)} %get-tuple-element.126) | copy-start | bytes 393220
  132.4 12.9 %copy-start.20 = (bf16[4,128,1,1,128]{4,1,0,3,2:T(8,128)(2,1)}, bf16[4,128,1,1,128]{4,1,0,3,2:T(8,128)(2,1)S(1)}, u32[]{:S(2)}) copy-start(bf16[4,128,1,1,128]{4,1,0,3,2:T(8,128)(2,1)S(1)} %get-tuple-element.125) | copy-start | bytes 393220
  132.4 1.6 copy-start.34
  132.7 0.8 copy-start.16
  132.8 1.7 copy-start.29
  132.8 1.7 copy-start.33
  134.0 3.3 copy-start.11
  137.3 5.2 %copy-start.8 = (bf16[16,128,1,1,128]{4,1,0,3,2:T(8,128)(2,1)}, bf16[16,128,1,1,128]{4,1,0,3,2:T(8,128)(2,1)S(1)}, u32[]{:S(2)}) copy-start(bf16[16,128,1,1,128]{4,1,0,3,2:T(8,128)(2,1)S(1)} %copy.173) | copy-start | bytes 1572868
  140.1 1.6 copy-start.19
  143.3 1.3 copy-start
  143.3 2.2 copy-start.45
  143.3 2.2 copy-start.46
  156.2 33.0 %all-to-all-start.3 = ((bf16[16,2,8192]{2,1,0:T(2,128)(2,1)}), bf16[16,2,8192]{2,1,0:T(2,128)(2,1)}, u32[]{:S(2)}, u32[]{:S(2)}) async-start(bf16[16,2,8192]{2,1,0:T(2,128)(2,1)} %reshape.1005), calls=%async_computation.3 | async-start | bytes 1048576 | tf_op jit(solution)/shard_map/all_to_all | solution.py:167
  162.8 1.8 copy-start.39
  164.2 1.6 copy-start.41
  164.3 1.8 copy-start.35
  164.7 47.0 %copy-start.6 = (bf16[2048,1,128]{2,0,1:T(8,128)(2,1)}, bf16[2048,1,128]{2,0,1:T(8,128)(2,1)S(1)}, u32[]{:S(2)}) copy-start(bf16[2048,1,128]{2,0,1:T(8,128)(2,1)S(1)} %fusion.44) | copy-start | bytes 1572868
  164.7 2.9 copy-start.37
  165.0 0.8 copy-start.14
  166.5 1.0 copy-start.12
  169.4 42.7 %copy-start.30 = (f32[128,128]{1,0:T(8,128)}, f32[128,128]{1,0:T(8,128)S(1)}, u32[]{:S(2)}) copy-start(f32[128,128]{1,0:T(8,128)S(1)} %fusion.46) | copy-start | bytes 196612
  190.9 36.8 %all-to-all-start.6 = ((f32[32,1,128,128]{3,2,1,0:T(8,128)}), f32[32,1,128,128]{3,2,1,0:T(8,128)}, u32[]{:S(2)}, u32[]{:S(2)}) async-start(f32[32,1,128,128]{3,2,1,0:T(8,128)} %broadcast_in_dim.71), calls=%async_computation.6 | async-start | bytes 4194304 | tf_op jit(solution)/shard_map/all_to_all | solution.py:36
  198.9 2.9 copy-start.18
  201.9 1.2 copy-start.4
  203.0 2.3 copy-start.9
  203.9 1.3 copy-start.2
  206.0 5.7 %copy-start.17 = (bf16[512,512]{1,0:T(8,128)(2,1)S(1)}, bf16[512,512]{1,0:T(8,128)(2,1)}, u32[]{:S(2)}) copy-start(bf16[512,512]{1,0:T(8,128)(2,1)} %copy-done.16) | copy-start | bytes 1572868
  227.7 40.4 %all-to-all-start.5 = ((bf16[16,2,8192]{2,1,0:T(2,128)(2,1)}), bf16[16,2,8192]{2,1,0:T(2,128)(2,1)}, u32[]{:S(2)}, u32[]{:S(2)}) async-start(bf16[16,2,8192]{2,1,0:T(2,128)(2,1)} %reshape.1007), calls=%async_computation.5 | async-start | bytes 1048576 | tf_op jit(solution)/shard_map/all_to_all | solution.py:168
  234.1 27.4 %copy-start.7 = (bf16[2048,1,128]{2,0,1:T(8,128)(2,1)S(1)}, bf16[2048,1,128]{2,0,1:T(8,128)(2,1)}, u32[]{:S(2)}) copy-start(bf16[2048,1,128]{2,0,1:T(8,128)(2,1)} %copy-done.6) | copy-start | bytes 1572868
  261.5 1.6 copy-start.1
  263.6 1.8 copy-start.31
  263.6 1.8 copy-start.32
  263.6 1.9 copy-start.10
  265.8 14.2 %copy-start.15 = (bf16[512,512]{1,0:T(8,128)(2,1)S(1)}, bf16[512,512]{1,0:T(8,128)(2,1)}, u32[]{:S(2)}) copy-start(bf16[512,512]{1,0:T(8,128)(2,1)} %copy-done.14) | copy-start | bytes 1572868
  265.8 14.2 %copy-start.27 = (bf16[4,128,1,1,128]{4,1,0,3,2:T(8,128)(2,1)S(1)}, bf16[4,128,1,1,128]{4,1,0,3,2:T(8,128)(2,1)}, u32[]{:S(2)}) copy-start(bf16[4,128,1,1,128]{4,1,0,3,2:T(8,128)(2,1)} %copy-done.26) | copy-start | bytes 393220
  267.2 13.4 %copy-start.13 = (bf16[512,1024]{1,0:T(8,128)(2,1)S(1)}, bf16[512,1024]{1,0:T(8,128)(2,1)}, u32[]{:S(2)}) copy-start(bf16[512,1024]{1,0:T(8,128)(2,1)} %copy-done.12) | copy-start | bytes 3145732
  267.2 13.4 %copy-start.25 = (bf16[4,128,1,1,128]{4,1,0,3,2:T(8,128)(2,1)S(1)}, bf16[4,128,1,1,128]{4,1,0,3,2:T(8,128)(2,1)}, u32[]{:S(2)}) copy-start(bf16[4,128,1,1,128]{4,1,0,3,2:T(8,128)(2,1)} %copy-done.24) | copy-start | bytes 393220
  268.1 35.6 %all-to-all-start.8 = ((bf16[16,2,8192]{2,1,0:T(2,128)(2,1)}), bf16[16,2,8192]{2,1,0:T(2,128)(2,1)S(1)}, u32[]{:S(2)}, u32[]{:S(2)}) async-start(bf16[16,2,8192]{2,1,0:T(2,128)(2,1)} %reshape.1011), calls=%async_computation.8 | async-start | bytes 1048576 | tf_op jit(solution)/shard_map/all_to_all | solution.py:170
  280.1 1.4 copy-start.5
  280.1 1.4 copy-start.23
  281.5 1.6 copy-start.3
  281.5 1.6 copy-start.21
  303.7 33.7 %all-to-all-start.7 = ((bf16[16,2,8192]{2,1,0:T(2,128)(2,1)}), bf16[16,2,8192]{2,1,0:T(2,128)(2,1)S(1)}, u32[]{:S(2)}, u32[]{:S(2)}) async-start(bf16[16,2,8192]{2,1,0:T(2,128)(2,1)} %reshape.1009), calls=%async_computation.7 | async-start | bytes 1048576 | tf_op jit(solution)/shard_map/all_to_all | solution.py:169
where the time goes:
time: 341 us; the launch traced here: 339 us
  waiting for transfers between devices  127 us (37%)
  starting transfers between devices  83.6 us (25%)
  blocking collectives  55.8 us (16%)
  local copies, waits for them, and re-layouts  40.1 us (12%)
  matrix products  21.2 us (6%)
  other arithmetic  9.61 us (3%)
    all_gather x6, blocking collectives, prefix_by_axis(): pieces = jax.tree.map(lambda part: lax.all_gather(part, axis), so_far)  55.8 us
    unnamed x115, local copies, waits for them, and re-layouts  28.3 us
    all_to_all x1, waiting for transfers between devices, shards(): lax.all_to_all(split_heads(values, group_count), 'head', split_axis=1, co...  26.4 us
    all_to_all x1, waiting for transfers between devices, shards(): lax.all_to_all(split_heads(keys, group_count), 'head', split_axis=1, conc...  26.1 us
    all_to_all x1, waiting for transfers between devices, shards(): lax.all_to_all(results[0], 'head', split_axis=0, concat_axis=1, tiled=True)  19.9 us
    all_to_all x1, waiting for transfers between devices, shards(): lax.all_to_all(results[3], 'head', split_axis=0, concat_axis=1, tiled=True)  17.6 us
    all_to_all x1, waiting for transfers between devices, shards(): lax.all_to_all(results[2], 'head', split_axis=0, concat_axis=1, tiled=True)  17.2 us
    all_to_all x1, starting transfers between devices, shards(): lax.all_to_all(split_heads(keys, group_count), 'head', split_axis=1, conc...  14.9 us
  transfers between devices with their start and end apart: 9, of which 7 were waited for; matrix products, arithmetic and copies ran while one was open for 17% of the time, Pallas kernels for 0%

commit v1 on v0

v1 whole, which is shorter than its diff:
```python
import jax
import jax.numpy as jnp
from jax import lax
from jax.experimental import pallas as pl
from jax.experimental.pallas import tpu as pltpu
from jax.sharding import PartitionSpec as P

HEADS = 16
DH = 128
ROWS = 128
F32 = jnp.float32
BF16 = jnp.bfloat16
MESH = pl.DeviceIdType.MESH


def position_scale(span, z):
    first = (span * 16 + z) * ROWS
    position = first + lax.broadcasted_iota(jnp.int32, (ROWS, 1), 0)
    return 1.0 / jnp.sqrt(jnp.float32(DH) * (position + 1).astype(F32))


def dot(a, b, dims):
    return lax.dot_general(a, b, (dims, ((), ())), preferred_element_type=F32)


def state_kernel(
    q_ref, k_ref, v_ref, g_ref, fin,
    scaled, abuf, rbuf, cbuf, xy, cs, fout, tot, tot_in,
    a_ss, a_rs, c_ss, c_rs, f_ss, f_rs, t_ss, t_rs,
):
    span, z = lax.axis_index("span"), lax.axis_index("head")
    chip, core = span // 2, span % 2
    x, y = chip // 4, chip % 4
    pair, member = z // 2, z % 2
    half = span // 16

    barrier = pltpu.get_barrier_semaphore()

    def signal(s, zz):
        pl.semaphore_signal(barrier, inc=1, device_id={"span": s, "head": zz}, device_id_type=MESH)

    def greet(i, carry):
        signal(lax.rem(span + i, 32), z)
        signal(lax.rem(span + i, 32), pair * 2 + 1 - member)
        return carry

    lax.fori_loop(1, 32, greet, 0)
    signal(span, pair * 2 + 1 - member)

    signal(span, lax.rem(z + 2, 16))
    signal(span, lax.rem(z + 14, 16))

    scaled[...] = (g_ref[...].astype(F32) * position_scale(span, z)).astype(BF16)
    pl.semaphore_wait(barrier, 65)

    my_slot = span % 16
    home = pair * 2 + half

    def send_state(owner):
        copy = pltpu.make_async_remote_copy(
            abuf.at[owner], rbuf.at[my_slot, member], a_ss.at[owner], a_rs.at[my_slot, member],
            device_id={"span": owner, "head": home}, device_id_type=MESH,
        )
        mine = jnp.logical_and(owner == span, home == z)

        @pl.when(mine)
        def _():
            rbuf[my_slot, member] = abuf[owner]

        @pl.when(jnp.logical_not(mine))
        def _():
            copy.start()

    def states(t, carry):
        head = lax.rem(x + t % 4, 4) * 4 + lax.rem(y + t // 4, 4)
        cols = pl.ds(pl.multiple_of(head * DH, DH), DH)
        abuf[head * 2] = dot(k_ref[:, cols], v_ref[:, cols], ((0,), (0,))).astype(BF16)
        send_state(head * 2)
        abuf[head * 2 + 1] = dot(scaled[:, cols], q_ref[:, cols], ((0,), (0,))).astype(BF16)
        send_state(head * 2 + 1)
        return carry

    lax.fori_loop(0, 16, states, 0)

    def slot_of(n):
        m, cc = n // 2, n % 2
        return ((m % 2) * 4 + lax.rem(y + 4 - m // 2, 4)) * 2 + cc

    def prepare(n):
        slot = slot_of(n)
        for par in range(2):
            mine = jnp.logical_and(slot + member * 16 == span, member == par)

            @pl.when(jnp.logical_not(mine))
            def _():
                pltpu.make_async_remote_copy(
                    abuf.at[0], rbuf.at[slot, par], a_ss.at[0], a_rs.at[slot, par],
                    device_id={"span": span, "head": pair * 2 + 1 - member}, device_id_type=MESH,
                ).wait_recv()
        cbuf[slot] = rbuf[slot, 0].astype(F32) + rbuf[slot, 1].astype(F32)

    def chain_copy(way, slot):
        return pltpu.make_async_remote_copy(
            cs.at[way, slot], xy.at[way, slot], c_ss.at[way, slot], c_rs.at[way, slot],
            device_id={"span": span, "head": (jnp.minimum(z + 2, 15) if way == 0 else jnp.maximum(z - 2, 0))},
            device_id_type=MESH,
        )

    def link(way, n):
        slot = slot_of(n)
        copy = chain_copy(way, slot)
        opens = pair == (0 if way == 0 else 7)
        ends = pair == (7 if way == 0 else 0)

        @pl.when(opens)
        def _():
            xy[way, slot] = jnp.zeros((DH, DH), BF16)
            cs[way, slot] = cbuf[slot].astype(BF16)

        @pl.when(jnp.logical_not(opens))
        def _():
            copy.wait_recv()

            @pl.when(jnp.logical_not(ends))
            def _():
                cs[way, slot] = (xy[way, slot].astype(F32) + cbuf[slot]).astype(BF16)

        @pl.when(jnp.logical_not(ends))
        def _():
            copy.start()

    up_lag = jnp.maximum(0, (2 * pair - 7) * 7 // 4)
    down_lag = jnp.maximum(0, (7 - 2 * pair) * 7 // 4)

    def step(t, carry):
        @pl.when(t < 16)
        def _():
            prepare(t)

        for way, lag in ((0, up_lag), (1, down_lag)):
            n = t - lag

            @pl.when(jnp.logical_and(n >= 0, n < 16))
            def _():
                link(way, jnp.clip(n, 0, 15))

        return carry

    lax.fori_loop(0, 16 + 12, step, 0)

    def add_total(i, acc):
        return acc + xy[0, i].astype(F32) + cbuf[i] + xy[1, i].astype(F32)

    gives = member == core
    tot_copy = pltpu.make_async_remote_copy(
        tot, tot_in, t_ss, t_rs, device_id={"span": span, "head": pair * 2 + 1 - member}, device_id_type=MESH,
    )

    @pl.when(gives)
    def _():
        tot[...] = lax.fori_loop(0, 16, add_total, jnp.zeros((DH, DH), F32))
        tot_copy.start()
        tot_in[...] = jnp.zeros((DH, DH), F32)

    @pl.when(jnp.logical_not(gives))
    def _():
        tot_copy.wait_recv()

    def prefix(i, before):
        idx = core * 15 + (1 - 2 * core) * i
        near = before + xy[core, idx].astype(F32)
        fout[idx, core] = near.astype(BF16)
        fout[idx, 1 - core] = (near + rbuf[idx, core].astype(F32)).astype(BF16)
        return before + xy[0, idx].astype(F32) + cbuf[idx] + xy[1, idx].astype(F32)

    lax.fori_loop(0, 16, prefix, tot_in[...])

    def back_copy(slot, par):
        return pltpu.make_async_remote_copy(
            fout.at[slot, par], fin.at[span], f_ss.at[slot, par], f_rs.at[span],
            device_id={"span": member * 16 + slot, "head": pair * 2 + par}, device_id_type=MESH,
        )

    def returns(t, carry):
        m, cc = t // 2, t % 2
        slot = (lax.rem(m + x, 2) * 4 + lax.rem(y + m // 2, 4)) * 2 + cc
        for par in range(2):
            mine = jnp.logical_and(slot + member * 16 == span, member == par)

            @pl.when(mine)
            def _():
                fin[span] = fout[slot, par]

            @pl.when(jnp.logical_not(mine))
            def _():
                back_copy(slot, par).start()

        return carry

    lax.fori_loop(0, 16, returns, 0)

    def arrive(o, carry):
        mine = jnp.logical_and(o == span, home == z)

        @pl.when(jnp.logical_not(mine))
        def _():
            pltpu.make_async_remote_copy(
                fout.at[0, 0], fin.at[o], f_ss.at[0, 0], f_rs.at[o],
                device_id={"span": span, "head": pair * 2 + 1 - member}, device_id_type=MESH,
            ).wait_recv()

            pltpu.make_async_remote_copy(
                abuf.at[o], rbuf.at[0, 0], a_ss.at[o], a_rs.at[0, 0],
                device_id={"span": span, "head": pair * 2 + 1 - member}, device_id_type=MESH,
            ).wait_send()

        return carry

    lax.fori_loop(0, 32, arrive, 0)

    def drain(i, carry):
        for par in range(2):
            mine = jnp.logical_and(i + member * 16 == span, member == par)

            @pl.when(jnp.logical_not(mine))
            def _():
                back_copy(i, par).wait_send()

        for way, ends in ((0, pair == 7), (1, pair == 0)):

            @pl.when(jnp.logical_not(ends))
            def _():
                chain_copy(way, i).wait_send()

        return carry

    lax.fori_loop(0, 16, drain, 0)

    @pl.when(gives)
    def _():
        tot_copy.wait_send()


def states_over_devices(q, k, v, g):
    dma = pltpu.SemaphoreType.DMA
    vmem = pl.BlockSpec(memory_space=pltpu.VMEM)
    return pl.pallas_call(
        state_kernel,
        out_shape=jax.ShapeDtypeStruct((32, DH, DH), BF16),
        in_specs=[vmem] * 4,
        out_specs=vmem,
        name="carried_states",
        scratch_shapes=[
            pltpu.VMEM((ROWS, HEADS * DH), BF16),
            pltpu.VMEM((32, DH, DH), BF16),
            pltpu.VMEM((16, 2, DH, DH), BF16),
            pltpu.VMEM((16, DH, DH), F32),
            pltpu.VMEM((2, 16, DH, DH), BF16),
            pltpu.VMEM((2, 16, DH, DH), BF16),
            pltpu.VMEM((16, 2, DH, DH), BF16),
            pltpu.VMEM((DH, DH), F32),
            pltpu.VMEM((DH, DH), F32),
            dma((32,)), dma((16, 2)),
            dma((2, 16)), dma((2, 16)),
            dma((16, 2)), dma((32,)),
            dma, dma,
        ],
        compiler_params=pltpu.CompilerParams(
            collective_id=0, has_side_effects=True, vmem_limit_bytes=32 << 20
        ),
    )(q, k, v, g)


STEP_HEADS = 4


def local_kernel(q_ref, k_ref, v_ref, g_ref, f_ref, out_ref, qg_ref, gk_ref, gv_ref):
    span, z = lax.axis_index("span"), lax.axis_index("head")
    scale = position_scale(span, z)
    row = lax.broadcasted_iota(jnp.int32, (ROWS, ROWS), 0)
    col = lax.broadcasted_iota(jnp.int32, (ROWS, ROWS), 1)
    causal = col <= row
    for i in range(STEP_HEADS):
        cols = slice(i * DH, (i + 1) * DH)
        q, k, v = q_ref[:, cols], k_ref[:, cols], v_ref[:, cols]
        s = (g_ref[:, cols].astype(F32) * scale).astype(BF16)
        fwd, back = f_ref[2 * i], f_ref[2 * i + 1]
        scores = jnp.where(causal, dot(q, k, ((1,), (1,))), 0.0).astype(BF16)
        dscores = jnp.where(causal, dot(s, v, ((1,), (1,))), 0.0).astype(BF16)
        out_ref[:, cols] = ((dot(scores, v, ((1,), (0,))) + dot(q, fwd, ((1,), (0,)))) * scale).astype(BF16)
        qg_ref[:, cols] = (dot(dscores, k, ((1,), (0,))) + dot(s, fwd, ((1,), (1,)))).astype(BF16)
        gk_ref[:, cols] = (dot(dscores, q, ((0,), (0,))) + dot(v, back, ((1,), (0,)))).astype(BF16)
        gv_ref[:, cols] = (dot(scores, s, ((0,), (0,))) + dot(k, back, ((1,), (1,)))).astype(BF16)


def local_terms(q, k, v, g, states):
    wide = pl.BlockSpec((ROWS, STEP_HEADS * DH), lambda i: (0, i))
    return pl.pallas_call(
        local_kernel,
        out_shape=[jax.ShapeDtypeStruct(q.shape, BF16)] * 4,
        grid=(HEADS // STEP_HEADS,),
        in_specs=[wide] * 4 + [pl.BlockSpec((2 * STEP_HEADS, DH, DH), lambda i: (i, 0, 0))],
        out_specs=[wide] * 4,
        name="chunk_terms",
        compiler_params=pltpu.CompilerParams(vmem_limit_bytes=32 << 20),
    )(q, k, v, g, states)


def shards(queries, keys, values, out_grad):
    states = states_over_devices(queries, keys, values, out_grad)
    return tuple(local_terms(queries, keys, values, out_grad, states))


def solution(mesh):
    placed = P(("span", "head"), None)
    return jax.shard_map(
        shards, mesh=mesh, in_specs=(placed,) * 4, out_specs=(placed,) * 4, check_vma=False
    )
```

time: 341 us -> 133 us (0.39)
  the two profiles are of different devices: /device:TPU:64 before, /device:TPU:7 now
where the time goes in v1:
time: 133 us
  Pallas kernels  128 us (96%)
  local copies, waits for them, and re-layouts  4.16 us (3%)
    pallas_call x1, Pallas kernels, states_over_devices(): pl.pallas_call(state_kernel, out_shape=jax.ShapeDtypeStruct((32, DH, DH),...  122 us
    pallas_call x1, Pallas kernels, local_terms(): pl.pallas_call(local_kernel, out_shape=[jax.ShapeDtypeStruct(q.shape, BF1...  5.26 us
    unnamed x8, local copies, waits for them, and re-layouts  4.16 us

profile of v1, /device:TPU:7, one launch (start us, length us, event | category | flops | bytes accessed | tf_op | source)
XLA Modules:
  0.0 132.5 jit_solution(3571044119270430321)
XLA Ops:
  0.6 0.0 copy-start
  0.6 1.0 copy-done
  1.7 0.0 copy-start.1
  1.7 1.0 copy-done.1
  2.7 0.0 copy-start.2
  2.7 1.0 copy-done.2
  3.8 0.0 copy-start.3
  3.8 1.0 copy-done.3
  4.8 122.4 %carried_states.1.f_ref = bf16[32,128,128]{2,1,0:T(8,128)(2,1)S(1)} custom-call(bf16[128,2048]{1,0:T(8,128)(2,1)S(1)} %copy-done, bf16[128,2048]{1,0:T(8,128)(2,1)S(1)} %copy-done.1, bf16[128,2048]{1,0:T(8,128)(2,1)S(1)} %copy-done.2, bf16[128,2048]{1,0:T(8,128)(2,1)S(1)} %copy-done.3), custom_call_target="tpu_custom_call" | custom-call | tf_op jit(solution)/shard_map/carried_states/pallas_call | solution.py:247
  127.2 5.3 %chunk_terms.1 = (bf16[128,2048]{1,0:T(8,128)(2,1)}, bf16[128,2048]{1,0:T(8,128)(2,1)}, bf16[128,2048]{1,0:T(8,128)(2,1)}, bf16[128,2048]{1,0:T(8,128)(2,1)}) custom-call(bf16[128,2048]{1,0:T(8,128)(2,1)S(1)} %copy-done, bf16[128,2048]{1,0:T(8,128)(2,1)S(1)} %copy-done.1, bf16[128,2048]{1,0:T(8,128)(2,1)S(1)} %copy-done.2, bf16[128,2048]{1,0:T(8,128)(2,1)S(1)} %copy-done.3, ...), custom_call_target="tpu_custom_call" | custom-call | tf_op jit(solution)/shard_map/chunk_terms/pallas_call | solution.py:298
Async XLA Ops:
  0.6 1.0 copy-start
  1.7 1.0 copy-start.1
  2.7 1.0 copy-start.2
  3.8 1.0 copy-start.3

commit v2 on v1

v2 whole, which is shorter than its diff:
```python
import jax
import jax.numpy as jnp
from jax import lax
from jax.experimental import pallas as pl
from jax.experimental.pallas import tpu as pltpu
from jax.sharding import PartitionSpec as P

HEADS = 16
DH = 128
ROWS = 128
F32 = jnp.float32
BF16 = jnp.bfloat16
MESH = pl.DeviceIdType.MESH


def position_scale(span, z):
    first = (span * 16 + z) * ROWS
    position = first + lax.broadcasted_iota(jnp.int32, (ROWS, 1), 0)
    return 1.0 / jnp.sqrt(jnp.float32(DH) * (position + 1).astype(F32))


def dot(a, b, dims):
    return lax.dot_general(a, b, (dims, ((), ())), preferred_element_type=F32)


SLICES = 2
PART = DH // SLICES
COUNT = 8 * SLICES
LAG = 8


def state_kernel(
    q_hbm, k_hbm, v_hbm, g_hbm, fin,
    q_ref, k_ref, v_ref, g_ref, abuf, rbuf, cbuf, xy, cs, fout, tot, tot_low, row_in, sum_low, sum_in,
    l_sem, a_ss, a_rs, c_ss, c_rs, f_ss, f_rs, t_ss, t_rs,
):
    span, z = lax.axis_index("span"), lax.axis_index("head")
    chip, core = span // 2, span % 2
    x, y = chip // 4, chip % 4
    pair, member = z // 2, z % 2
    gx, gy, lx, ly = x // 2, y // 2, x % 2, y % 2
    slot_me = (lx * 2 + ly) * 2 + core
    head_me = slot_me * 2 + member

    def place(slot):
        return ((gx * 2 + slot // 4) * 4 + gy * 2 + slot // 2 % 2) * 2 + slot % 2

    def turned(n):
        return (lx + n // 4) % 2 * 4 + (ly + n // 2) % 2 * 2 + (core + n) % 2

    loads = [
        pltpu.make_async_copy(src, dst, l_sem.at[i])
        for i, (src, dst) in enumerate(((k_hbm, k_ref), (v_hbm, v_ref), (g_hbm, g_ref), (q_hbm, q_ref)))
    ]
    for load in loads:
        load.start()

    barrier = pltpu.get_barrier_semaphore()

    def signal(s, zz):
        pl.semaphore_signal(barrier, inc=1, device_id={"span": s, "head": zz}, device_id_type=MESH)

    def greet(i, carry):
        signal(place(turned(i // 2)), pair * 2 + (member + i) % 2)
        return carry

    lax.fori_loop(1, 16, greet, 0)

    def group_span(px, py):
        return ((px * 2 + lx) * 4 + py * 2 + ly) * 2 + core

    partners = [group_span(gx, 1 - gy), group_span(1 - gx, gy), group_span(1 - gx, 1 - gy)]
    for s in partners:
        signal(s, z)
    signal(span, lax.rem(z + 2, 16))
    signal(span, lax.rem(z + 14, 16))

    scale = position_scale(span, z)
    for load in loads:
        load.wait()

    def head_of(t):
        return turned(t // 2) * 2 + (member + t) % 2

    def states(t, carry):
        head = head_of(t)
        cols = pl.ds(pl.multiple_of(head * DH, DH), DH)
        scaled = (g_ref[:, cols].astype(F32) * scale).astype(BF16)
        abuf[head, 0] = dot(k_ref[:, cols], v_ref[:, cols], ((0,), (0,))).astype(BF16)
        abuf[head, 1] = dot(scaled, q_ref[:, cols], ((0,), (0,))).astype(BF16)
        return carry

    lax.fori_loop(0, 16, states, 0, unroll=2)

    pl.semaphore_wait(barrier, 20)

    def rows(part):
        return pl.ds(pl.multiple_of(part * PART, PART), PART)

    def send_states(t, carry):
        head, part = head_of(t % 16), t // 16
        src, dst = abuf.at[head, :, rows(part)], rbuf.at[slot_me, member, :, rows(part)]
        mine = head == head_me

        @pl.when(mine)
        def _():
            pltpu.make_async_copy(src, dst, a_rs.at[slot_me, part]).start()

        @pl.when(jnp.logical_not(mine))
        def _():
            pltpu.make_async_remote_copy(
                src, dst, a_ss, a_rs.at[slot_me, part],
                device_id={"span": place(head // 2), "head": pair * 2 + head % 2}, device_id_type=MESH,
            ).start()

        return carry

    lax.fori_loop(0, 16 * SLICES, send_states, 0)

    def prepare(t):
        slot, part = turned(t % 8), t // 8
        both = rbuf.at[slot, :, :, rows(part)]
        pltpu.make_async_copy(both, both, a_rs.at[slot, part]).wait()
        cbuf[slot, :, rows(part)] = (
            rbuf[slot, 0, :, rows(part)].astype(F32) + rbuf[slot, 1, :, rows(part)].astype(F32)
        )

    def link(way, n):
        slot, part = turned(n % 8), n // 8
        at = (way, slot, slice(None), rows(part))
        copy = pltpu.make_async_remote_copy(
            cs.at[at], xy.at[at], c_ss.at[way], c_rs.at[way, slot, part],
            device_id={"span": span, "head": (jnp.minimum(z + 2, 15) if way == 0 else jnp.maximum(z - 2, 0))},
            device_id_type=MESH,
        )
        opens = pair == (0 if way == 0 else 7)
        ends = pair == (7 if way == 0 else 0)

        @pl.when(opens)
        def _():
            xy[at] = jnp.zeros((2, PART, DH), BF16)
            cs[at] = cbuf[slot, :, rows(part)].astype(BF16)
            copy.start()

        @pl.when(jnp.logical_not(opens))
        def _():
            copy.wait_recv()

            @pl.when(jnp.logical_not(ends))
            def _():
                cs[at] = (xy[at].astype(F32) + cbuf[slot, :, rows(part)]).astype(BF16)
                copy.start()

    up_lag = jnp.clip((2 * pair - 7) * LAG // 2, 0, COUNT)
    down_lag = jnp.clip((7 - 2 * pair) * LAG // 2, 0, COUNT)
    last_lag = jnp.maximum(up_lag, down_lag)

    def whole(slot, r):
        return xy[0, slot, :, r].astype(F32) + cbuf[slot, :, r] + xy[1, slot, :, r].astype(F32)

    def row_copy(part):
        return pltpu.make_async_remote_copy(
            tot_low.at[:, :, rows(part)], row_in.at[:, :, rows(part)], t_ss, t_rs.at[part],
            device_id={"span": partners[0], "head": z}, device_id_type=MESH,
        )

    def sum_copy(i, part):
        return pltpu.make_async_remote_copy(
            sum_low.at[rows(part)], sum_in.at[i - 1, rows(part)], t_ss, t_rs.at[part],
            device_id={"span": partners[i], "head": z}, device_id_type=MESH,
        )

    def offer(part):
        r = rows(part)
        tot_low[:, :, r] = tot[:, :, r].astype(BF16)
        sum_low[r] = jnp.where(gx == 0, tot[0, 0, r] + tot[0, 1, r], tot[1, 0, r] + tot[1, 1, r]).astype(BF16)
        row_copy(part).start()
        sum_copy(1, part).start()
        sum_copy(2, part).start()

    def finish(part):
        r = rows(part)
        six = cs.at[0, 0:3, :, r]
        pltpu.make_async_copy(six, six, t_rs.at[part]).wait()
        far = sum_in[0, r].astype(F32) + sum_in[1, r].astype(F32)
        later, first = gy == 1, gy == 0
        low = jnp.where(gx == 1, far, 0.0) + jnp.where(later, row_in[0, 0, r].astype(F32), 0.0)
        high = jnp.where(gx == 0, far, 0.0) + jnp.where(first, row_in[1, 1, r].astype(F32), 0.0)
        low_turn = jnp.where(later, row_in[0, 1, r], row_in[0, 0, r]).astype(F32)
        high_turn = jnp.where(first, row_in[1, 0, r], row_in[1, 1, r]).astype(F32)

        def prefix(i, before):
            low, high = before
            j = 7 - i
            near = low + xy[0, i, 0, r].astype(F32)
            fout[i, 0, 0, r] = near.astype(BF16)
            fout[i, 1, 0, r] = (near + rbuf[i, 0, 0, r].astype(F32)).astype(BF16)
            low = low + xy[0, i, 0, r].astype(F32) + cbuf[i, 0, r] + xy[1, i, 0, r].astype(F32)
            near = high + xy[1, j, 1, r].astype(F32)
            fout[j, 1, 1, r] = near.astype(BF16)
            fout[j, 0, 1, r] = (near + rbuf[j, 1, 1, r].astype(F32)).astype(BF16)
            high = high + xy[0, j, 1, r].astype(F32) + cbuf[j, 1, r] + xy[1, j, 1, r].astype(F32)
            return low, high

        low, high = lax.fori_loop(0, 4, prefix, (low, high), unroll=2)
        lax.fori_loop(4, 8, prefix, (low + low_turn, high + high_turn), unroll=2)

        def returns(t, carry):
            slot, par = turned(t // 2), (member + t) % 2
            src, dst = fout.at[slot, par, :, r], fin.at[head_me, :, r]
            mine = t == 0

            @pl.when(mine)
            def _():
                pltpu.make_async_copy(src, dst, f_rs).start()

            @pl.when(jnp.logical_not(mine))
            def _():
                pltpu.make_async_remote_copy(
                    src, dst, f_ss, f_rs,
                    device_id={"span": place(slot), "head": pair * 2 + par}, device_id_type=MESH,
                ).start()

            return carry

        lax.fori_loop(0, 16, returns, 0)

    def step(t, carry):
        @pl.when(t < COUNT)
        def _():
            prepare(t)

        for way, lag in ((0, up_lag), (1, down_lag)):
            n = t - lag

            @pl.when(jnp.logical_and(n >= 0, n < COUNT))
            def _():
                link(way, jnp.clip(n, 0, COUNT - 1))

        done = t - last_lag

        @pl.when(jnp.logical_and(done >= 0, done < COUNT))
        def _():
            at = jnp.clip(done, 0, COUNT - 1)
            part = at // 8
            r = rows(part)
            slot = turned(at % 8)
            tot[:, slot // 4, r] = tot[:, slot // 4, r] + whole(slot, r)

            @pl.when(at % 8 == 7)
            def _():
                offer(part)

        ready = done - 1

        @pl.when(jnp.logical_and(ready >= 7, jnp.logical_and(ready < COUNT, ready % 8 == 7)))
        def _():
            finish(jnp.clip(ready, 0, COUNT - 1) // 8)

        return carry

    tot[...] = jnp.zeros((2, 2, DH, DH), F32)
    lax.fori_loop(0, 2 * COUNT + 1, step, 0)

    pltpu.make_async_copy(fin, fin, f_rs).wait()

    most = abuf.at[pl.ds(0, 15)]
    pltpu.make_async_copy(most, most, a_ss).wait()
    pltpu.make_async_copy(most, most, f_ss).wait()

    for way, ends in ((0, pair == 7), (1, pair == 0)):

        @pl.when(jnp.logical_not(ends))
        def _():
            pltpu.make_async_copy(cs.at[way], cs.at[way], c_ss.at[way]).wait()

    pltpu.make_async_copy(cs.at[0, 0:3], cs.at[0, 0:3], t_ss).wait()


def states_over_devices(q, k, v, g):
    dma = pltpu.SemaphoreType.DMA
    return pl.pallas_call(
        state_kernel,
        out_shape=jax.ShapeDtypeStruct((16, 2, DH, DH), BF16),
        in_specs=[pl.BlockSpec(memory_space=pltpu.HBM)] * 4,
        out_specs=pl.BlockSpec(memory_space=pltpu.VMEM),
        name="carried_states",
        scratch_shapes=[pltpu.VMEM((ROWS, HEADS * DH), BF16)] * 4
        + [
            pltpu.VMEM((16, 2, DH, DH), BF16),
            pltpu.VMEM((8, 2, 2, DH, DH), BF16),
            pltpu.VMEM((8, 2, DH, DH), F32),
            pltpu.VMEM((2, 8, 2, DH, DH), BF16),
            pltpu.VMEM((2, 8, 2, DH, DH), BF16),
            pltpu.VMEM((8, 2, 2, DH, DH), BF16),
            pltpu.VMEM((2, 2, DH, DH), F32),
            pltpu.VMEM((2, 2, DH, DH), BF16),
            pltpu.VMEM((2, 2, DH, DH), BF16),
            pltpu.VMEM((DH, DH), BF16),
            pltpu.VMEM((2, DH, DH), BF16),
            dma((4,)),
            dma, dma((8, SLICES)),
            dma((2,)), dma((2, 8, SLICES)),
            dma, dma,
            dma, dma((SLICES,)),
        ],
        compiler_params=pltpu.CompilerParams(
            collective_id=0, has_side_effects=True, vmem_limit_bytes=56 << 20
        ),
    )(q, k, v, g)


STEP_HEADS = 4


def local_kernel(q_ref, k_ref, v_ref, g_ref, f_ref, out_ref, qg_ref, gk_ref, gv_ref):
    span, z = lax.axis_index("span"), lax.axis_index("head")
    scale = position_scale(span, z)
    row = lax.broadcasted_iota(jnp.int32, (ROWS, ROWS), 0)
    col = lax.broadcasted_iota(jnp.int32, (ROWS, ROWS), 1)
    causal = col <= row
    for i in range(STEP_HEADS):
        cols = slice(i * DH, (i + 1) * DH)
        q, k, v = q_ref[:, cols], k_ref[:, cols], v_ref[:, cols]
        s = (g_ref[:, cols].astype(F32) * scale).astype(BF16)
        head = pl.program_id(0) * STEP_HEADS + i
        fwd, back = f_ref[head, 0], f_ref[head, 1]
        scores = jnp.where(causal, dot(q, k, ((1,), (1,))), 0.0).astype(BF16)
        dscores = jnp.where(causal, dot(s, v, ((1,), (1,))), 0.0).astype(BF16)
        out_ref[:, cols] = ((dot(scores, v, ((1,), (0,))) + dot(q, fwd, ((1,), (0,)))) * scale).astype(BF16)
        qg_ref[:, cols] = (dot(dscores, k, ((1,), (0,))) + dot(s, fwd, ((1,), (1,)))).astype(BF16)
        gk_ref[:, cols] = (dot(dscores, q, ((0,), (0,))) + dot(v, back, ((1,), (0,)))).astype(BF16)
        gv_ref[:, cols] = (dot(scores, s, ((0,), (0,))) + dot(k, back, ((1,), (1,)))).astype(BF16)


def local_terms(q, k, v, g, states):
    wide = pl.BlockSpec((ROWS, STEP_HEADS * DH), lambda i: (0, i))
    return pl.pallas_call(
        local_kernel,
        out_shape=[jax.ShapeDtypeStruct(q.shape, BF16)] * 4,
        grid=(HEADS // STEP_HEADS,),
        in_specs=[wide] * 4 + [pl.BlockSpec(memory_space=pltpu.VMEM)],
        out_specs=[wide] * 4,
        name="chunk_terms",
        compiler_params=pltpu.CompilerParams(vmem_limit_bytes=32 << 20),
    )(q, k, v, g, states)


def shards(queries, keys, values, out_grad):
    states = states_over_devices(queries, keys, values, out_grad)
    return tuple(local_terms(queries, keys, values, out_grad, states))


def solution(mesh):
    placed = P(("span", "head"), None)
    return jax.shard_map(
        shards, mesh=mesh, in_specs=(placed,) * 4, out_specs=(placed,) * 4, check_vma=False
    )
```

time: 133 us -> 105 us (0.79)
  the two profiles are of different devices: /device:TPU:7 before, /device:TPU:1 now
where the time goes in v2:
time: 105 us; the launch traced here: 104 us
  Pallas kernels  102 us (97%)
  local copies, waits for them, and re-layouts  1.23 us (1%)
    pallas_call x1, Pallas kernels, states_over_devices(): pl.pallas_call(state_kernel, out_shape=jax.ShapeDtypeStruct((16, 2, DH, D...  97.2 us
    pallas_call x1, Pallas kernels, local_terms(): pl.pallas_call(local_kernel, out_shape=[jax.ShapeDtypeStruct(q.shape, BF1...  5.23 us

profile of v2, /device:TPU:1, one launch (start us, length us, event | category | flops | bytes accessed | tf_op | source)
XLA Modules:
  0.0 104.3 jit_solution(1592406490382848956)
XLA Ops:
  0.6 0.0 copy-start.4
  0.6 0.0 copy-start.3
  0.7 0.0 copy-start.2
  0.7 0.0 copy-start.1
  0.7 97.2 %carried_states.1.f_ref = bf16[16,2,128,128]{3,2,1,0:T(8,128)(2,1)} custom-call(bf16[128,2048]{1,0:T(8,128)(2,1)} %q_ref.1, bf16[128,2048]{1,0:T(8,128)(2,1)} %k_ref.1, bf16[128,2048]{1,0:T(8,128)(2,1)} %v_ref.1, bf16[128,2048]{1,0:T(8,128)(2,1)} %g_ref.1), custom_call_target="tpu_custom_call" | custom-call | tf_op jit(solution)/shard_map/carried_states/pallas_call | solution.py:282
  97.8 0.0 copy-done.4
  97.8 0.0 copy-done.3
  97.9 0.0 copy-done.2
  97.9 0.0 copy-done.1
  97.9 0.0 copy-start
  97.9 1.2 %copy-done = bf16[16,2,128,128]{3,2,1,0:T(8,128)(2,1)S(1)} copy-done((bf16[16,2,128,128]{3,2,1,0:T(8,128)(2,1)S(1)}, bf16[16,2,128,128]{3,2,1,0:T(8,128)(2,1)}, u32[]{:S(2)}) %copy-start) | copy-done | bytes 1048600
  99.1 5.2 %chunk_terms.1 = (bf16[128,2048]{1,0:T(8,128)(2,1)}, bf16[128,2048]{1,0:T(8,128)(2,1)}, bf16[128,2048]{1,0:T(8,128)(2,1)}, bf16[128,2048]{1,0:T(8,128)(2,1)}) custom-call(bf16[128,2048]{1,0:T(8,128)(2,1)S(1)} %copy-done.1, bf16[128,2048]{1,0:T(8,128)(2,1)S(1)} %copy-done.2, bf16[128,2048]{1,0:T(8,128)(2,1)S(1)} %copy-done.3, ...), custom_call_target="tpu_custom_call" | custom-call | tf_op jit(solution)/shard_map/chunk_terms/pallas_call | solution.py:338
Async XLA Ops:
  0.6 97.2 %copy-start.4 = (bf16[128,2048]{1,0:T(8,128)(2,1)S(1)}, bf16[128,2048]{1,0:T(8,128)(2,1)}, u32[]{:S(2)}) copy-start(bf16[128,2048]{1,0:T(8,128)(2,1)} %g_ref.1) | copy-start | bytes 1572868
  0.6 97.2 %copy-start.3 = (bf16[128,2048]{1,0:T(8,128)(2,1)S(1)}, bf16[128,2048]{1,0:T(8,128)(2,1)}, u32[]{:S(2)}) copy-start(bf16[128,2048]{1,0:T(8,128)(2,1)} %v_ref.1) | copy-start | bytes 1572868
  0.7 97.2 %copy-start.2 = (bf16[128,2048]{1,0:T(8,128)(2,1)S(1)}, bf16[128,2048]{1,0:T(8,128)(2,1)}, u32[]{:S(2)}) copy-start(bf16[128,2048]{1,0:T(8,128)(2,1)} %k_ref.1) | copy-start | bytes 1572868
  0.7 97.2 %copy-start.1 = (bf16[128,2048]{1,0:T(8,128)(2,1)S(1)}, bf16[128,2048]{1,0:T(8,128)(2,1)}, u32[]{:S(2)}) copy-start(bf16[128,2048]{1,0:T(8,128)(2,1)} %q_ref.1) | copy-start | bytes 1572868
  97.9 1.2 %copy-start = (bf16[16,2,128,128]{3,2,1,0:T(8,128)(2,1)S(1)}, bf16[16,2,128,128]{3,2,1,0:T(8,128)(2,1)}, u32[]{:S(2)}) copy-start(bf16[16,2,128,128]{3,2,1,0:T(8,128)(2,1)} %carried_states.1.f_ref) | copy-start | bytes 3145732

commit v3 on v2

--- a/solution.py
+++ b/solution.py
@@ -31,22 +31,24 @@
 
 def state_kernel(
     q_hbm, k_hbm, v_hbm, g_hbm, fin,
-    q_ref, k_ref, v_ref, g_ref, abuf, rbuf, cbuf, xy, cs, fout, tot, tot_low, row_in, sum_low, sum_in,
+    q_ref, k_ref, v_ref, g_ref, abuf, rbuf, xy, cs, fout, tot, tot_low, row_in, sum_low, sum_in,
     l_sem, a_ss, a_rs, c_ss, c_rs, f_ss, f_rs, t_ss, t_rs,
 ):
     span, z = lax.axis_index("span"), lax.axis_index("head")
-    chip, core = span // 2, span % 2
-    x, y = chip // 4, chip % 4
-    pair, member = z // 2, z % 2
-    gx, gy, lx, ly = x // 2, y // 2, x % 2, y % 2
+    chip, core = span >> 1, span & 1
+    x, y = chip >> 2, chip & 3
+    pair, member = z >> 1, z & 1
+    gx, gy, lx, ly = x >> 1, y >> 1, x & 1, y & 1
     slot_me = (lx * 2 + ly) * 2 + core
     head_me = slot_me * 2 + member
 
+    corner = gx * 16 + gy * 4
+
     def place(slot):
-        return ((gx * 2 + slot // 4) * 4 + gy * 2 + slot // 2 % 2) * 2 + slot % 2
+        return corner + (slot >> 2) * 8 + (slot & 3)
 
     def turned(n):
-        return (lx + n // 4) % 2 * 4 + (ly + n // 2) % 2 * 2 + (core + n) % 2
+        return slot_me ^ n
 
     loads = [
         pltpu.make_async_copy(src, dst, l_sem.at[i])
@@ -61,7 +63,7 @@
         pl.semaphore_signal(barrier, inc=1, device_id={"span": s, "head": zz}, device_id_type=MESH)
 
     def greet(i, carry):
-        signal(place(turned(i // 2)), pair * 2 + (member + i) % 2)
+        signal(place(turned(i >> 1)), pair * 2 + (member ^ (i & 1)))
         return carry
 
     lax.fori_loop(1, 16, greet, 0)
@@ -80,7 +82,7 @@
         load.wait()
 
     def head_of(t):
-        return turned(t // 2) * 2 + (member + t) % 2
+        return head_me ^ t
 
     def states(t, carry):
         head = head_of(t)
@@ -98,7 +100,7 @@
         return pl.ds(pl.multiple_of(part * PART, PART), PART)
 
     def send_states(t, carry):
-        head, part = head_of(t % 16), t // 16
+        head, part = head_of(t & 15), t >> 4
         src, dst = abuf.at[head, :, rows(part)], rbuf.at[slot_me, member, :, rows(part)]
         mine = head == head_me
 
@@ -110,7 +112,7 @@
         def _():
             pltpu.make_async_remote_copy(
                 src, dst, a_ss, a_rs.at[slot_me, part],
-                device_id={"span": place(head // 2), "head": pair * 2 + head % 2}, device_id_type=MESH,
+                device_id={"span": place(head >> 1), "head": pair * 2 + (head & 1)}, device_id_type=MESH,
             ).start()
 
         return carry
@@ -118,15 +120,15 @@
     lax.fori_loop(0, 16 * SLICES, send_states, 0)
 
     def prepare(t):
-        slot, part = turned(t % 8), t // 8
+        slot, part = turned(t & 7), t >> 3
         both = rbuf.at[slot, :, :, rows(part)]
         pltpu.make_async_copy(both, both, a_rs.at[slot, part]).wait()
-        cbuf[slot, :, rows(part)] = (
-            rbuf[slot, 0, :, rows(part)].astype(F32) + rbuf[slot, 1, :, rows(part)].astype(F32)
-        )
+
+    def both_chunks(slot, r):
+        return rbuf[slot, 0, :, r].astype(F32) + rbuf[slot, 1, :, r].astype(F32)
 
     def link(way, n):
-        slot, part = turned(n % 8), n // 8
+        slot, part = turned(n & 7), n >> 3
         at = (way, slot, slice(None), rows(part))
         copy = pltpu.make_async_remote_copy(
             cs.at[at], xy.at[at], c_ss.at[way], c_rs.at[way, slot, part],
@@ -139,7 +141,7 @@
         @pl.when(opens)
         def _():
             xy[at] = jnp.zeros((2, PART, DH), BF16)
-            cs[at] = cbuf[slot, :, rows(part)].astype(BF16)
+            cs[at] = both_chunks(slot, rows(part)).astype(BF16)
             copy.start()
 
         @pl.when(jnp.logical_not(opens))
@@ -148,15 +150,15 @@
 
             @pl.when(jnp.logical_not(ends))
             def _():
-                cs[at] = (xy[at].astype(F32) + cbuf[slot, :, rows(part)]).astype(BF16)
+                cs[at] = (xy[at].astype(F32) + both_chunks(slot, rows(part))).astype(BF16)
                 copy.start()
 
-    up_lag = jnp.clip((2 * pair - 7) * LAG // 2, 0, COUNT)
-    down_lag = jnp.clip((7 - 2 * pair) * LAG // 2, 0, COUNT)
+    up_lag = jnp.clip(((2 * pair - 7) * LAG) >> 1, 0, COUNT)
+    down_lag = jnp.clip(((7 - 2 * pair) * LAG) >> 1, 0, COUNT)
     last_lag = jnp.maximum(up_lag, down_lag)
 
     def whole(slot, r):
-        return xy[0, slot, :, r].astype(F32) + cbuf[slot, :, r] + xy[1, slot, :, r].astype(F32)
+        return xy[0, slot, :, r].astype(F32) + both_chunks(slot, r) + xy[1, slot, :, r].astype(F32)
 
     def row_copy(part):
         return pltpu.make_async_remote_copy(
@@ -194,19 +196,21 @@
             j = 7 - i
             near = low + xy[0, i, 0, r].astype(F32)
             fout[i, 0, 0, r] = near.astype(BF16)
-            fout[i, 1, 0, r] = (near + rbuf[i, 0, 0, r].astype(F32)).astype(BF16)
-            low = low + xy[0, i, 0, r].astype(F32) + cbuf[i, 0, r] + xy[1, i, 0, r].astype(F32)
+            near = near + rbuf[i, 0, 0, r].astype(F32)
+            fout[i, 1, 0, r] = near.astype(BF16)
+            low = near + rbuf[i, 1, 0, r].astype(F32) + xy[1, i, 0, r].astype(F32)
             near = high + xy[1, j, 1, r].astype(F32)
             fout[j, 1, 1, r] = near.astype(BF16)
-            fout[j, 0, 1, r] = (near + rbuf[j, 1, 1, r].astype(F32)).astype(BF16)
-            high = high + xy[0, j, 1, r].astype(F32) + cbuf[j, 1, r] + xy[1, j, 1, r].astype(F32)
+            near = near + rbuf[j, 1, 1, r].astype(F32)
+            fout[j, 0, 1, r] = near.astype(BF16)
+            high = near + rbuf[j, 0, 1, r].astype(F32) + xy[0, j, 1, r].astype(F32)
             return low, high
 
         low, high = lax.fori_loop(0, 4, prefix, (low, high), unroll=2)
         lax.fori_loop(4, 8, prefix, (low + low_turn, high + high_turn), unroll=2)
 
         def returns(t, carry):
-            slot, par = turned(t // 2), (member + t) % 2
+            slot, par = turned(t >> 1), member ^ (t & 1)
             src, dst = fout.at[slot, par, :, r], fin.at[head_me, :, r]
             mine = t == 0
 
@@ -242,20 +246,20 @@
         @pl.when(jnp.logical_and(done >= 0, done < COUNT))
         def _():
             at = jnp.clip(done, 0, COUNT - 1)
-            part = at // 8
+            part = at >> 3
             r = rows(part)
-            slot = turned(at % 8)
-            tot[:, slot // 4, r] = tot[:, slot // 4, r] + whole(slot, r)
-
-            @pl.when(at % 8 == 7)
+            slot = turned(at & 7)
+            tot[:, slot >> 2, r] = tot[:, slot >> 2, r] + whole(slot, r)
+
+            @pl.when(at & 7 == 7)
             def _():
                 offer(part)
 
         ready = done - 1
 
-        @pl.when(jnp.logical_and(ready >= 7, jnp.logical_and(ready < COUNT, ready % 8 == 7)))
-        def _():
-            finish(jnp.clip(ready, 0, COUNT - 1) // 8)
+        @pl.when(jnp.logical_and(ready >= 7, jnp.logical_and(ready < COUNT, ready & 7 == 7)))
+        def _():
+            finish(jnp.clip(ready, 0, COUNT - 1) >> 3)
 
         return carry
 
@@ -289,7 +293,6 @@
         + [
             pltpu.VMEM((16, 2, DH, DH), BF16),
             pltpu.VMEM((8, 2, 2, DH, DH), BF16),
-            pltpu.VMEM((8, 2, DH, DH), F32),
             pltpu.VMEM((2, 8, 2, DH, DH), BF16),
             pltpu.VMEM((2, 8, 2, DH, DH), BF16),
             pltpu.VMEM((8, 2, 2, DH, DH), BF16),

time: 105 us -> 104 us (level)
  no operation moved by 1% of the time
where the time goes in v3:
time: 104 us; the launch traced here: 103 us
  Pallas kernels  101 us (97%)
  local copies, waits for them, and re-layouts  1.23 us (1%)
    pallas_call x1, Pallas kernels, states_over_devices(): pl.pallas_call(state_kernel, out_shape=jax.ShapeDtypeStruct((16, 2, DH, D...  96.2 us
    pallas_call x1, Pallas kernels, local_terms(): pl.pallas_call(local_kernel, out_shape=[jax.ShapeDtypeStruct(q.shape, BF1...  5.23 us

profile of v3, /device:TPU:1, one launch (start us, length us, event | category | flops | bytes accessed | tf_op | source)
XLA Modules:
  0.0 103.4 jit_solution(12426976321095316490)
XLA Ops:
  0.6 0.0 copy-start.4
  0.6 0.0 copy-start.3
  0.7 0.0 copy-start.2
  0.7 0.0 copy-start.1
  0.7 96.2 %carried_states.1.f_ref = bf16[16,2,128,128]{3,2,1,0:T(8,128)(2,1)} custom-call(bf16[128,2048]{1,0:T(8,128)(2,1)} %q_ref.1, bf16[128,2048]{1,0:T(8,128)(2,1)} %k_ref.1, bf16[128,2048]{1,0:T(8,128)(2,1)} %v_ref.1, bf16[128,2048]{1,0:T(8,128)(2,1)} %g_ref.1), custom_call_target="tpu_custom_call" | custom-call | tf_op jit(solution)/shard_map/carried_states/pallas_call | solution.py:286
  96.9 0.0 copy-done.4
  96.9 0.0 copy-done.3
  96.9 0.0 copy-done.2
  96.9 0.0 copy-done.1
  96.9 0.0 copy-start
  96.9 1.2 %copy-done = bf16[16,2,128,128]{3,2,1,0:T(8,128)(2,1)S(1)} copy-done((bf16[16,2,128,128]{3,2,1,0:T(8,128)(2,1)S(1)}, bf16[16,2,128,128]{3,2,1,0:T(8,128)(2,1)}, u32[]{:S(2)}) %copy-start) | copy-done | bytes 1048600
  98.1 5.2 %chunk_terms.1 = (bf16[128,2048]{1,0:T(8,128)(2,1)}, bf16[128,2048]{1,0:T(8,128)(2,1)}, bf16[128,2048]{1,0:T(8,128)(2,1)}, bf16[128,2048]{1,0:T(8,128)(2,1)}) custom-call(bf16[128,2048]{1,0:T(8,128)(2,1)S(1)} %copy-done.1, bf16[128,2048]{1,0:T(8,128)(2,1)S(1)} %copy-done.2, bf16[128,2048]{1,0:T(8,128)(2,1)S(1)} %copy-done.3, ...), custom_call_target="tpu_custom_call" | custom-call | tf_op jit(solution)/shard_map/chunk_terms/pallas_call | solution.py:341
Async XLA Ops:
  0.6 96.3 %copy-start.4 = (bf16[128,2048]{1,0:T(8,128)(2,1)S(1)}, bf16[128,2048]{1,0:T(8,128)(2,1)}, u32[]{:S(2)}) copy-start(bf16[128,2048]{1,0:T(8,128)(2,1)} %g_ref.1) | copy-start | bytes 1572868
  0.6 96.3 %copy-start.3 = (bf16[128,2048]{1,0:T(8,128)(2,1)S(1)}, bf16[128,2048]{1,0:T(8,128)(2,1)}, u32[]{:S(2)}) copy-start(bf16[128,2048]{1,0:T(8,128)(2,1)} %v_ref.1) | copy-start | bytes 1572868
  0.7 96.3 %copy-start.2 = (bf16[128,2048]{1,0:T(8,128)(2,1)S(1)}, bf16[128,2048]{1,0:T(8,128)(2,1)}, u32[]{:S(2)}) copy-start(bf16[128,2048]{1,0:T(8,128)(2,1)} %k_ref.1) | copy-start | bytes 1572868
  0.7 96.3 %copy-start.1 = (bf16[128,2048]{1,0:T(8,128)(2,1)S(1)}, bf16[128,2048]{1,0:T(8,128)(2,1)}, u32[]{:S(2)}) copy-start(bf16[128,2048]{1,0:T(8,128)(2,1)} %q_ref.1) | copy-start | bytes 1572868
  96.9 1.2 %copy-start = (bf16[16,2,128,128]{3,2,1,0:T(8,128)(2,1)S(1)}, bf16[16,2,128,128]{3,2,1,0:T(8,128)(2,1)}, u32[]{:S(2)}) copy-start(bf16[16,2,128,128]{3,2,1,0:T(8,128)(2,1)} %carried_states.1.f_ref) | copy-start | bytes 3145732

commit v4 on v3

--- a/solution.py
+++ b/solution.py
@@ -255,7 +255,7 @@
             def _():
                 offer(part)
 
-        ready = done - 1
+        ready = done - 9
 
         @pl.when(jnp.logical_and(ready >= 7, jnp.logical_and(ready < COUNT, ready & 7 == 7)))
         def _():
@@ -264,7 +264,7 @@
         return carry
 
     tot[...] = jnp.zeros((2, 2, DH, DH), F32)
-    lax.fori_loop(0, 2 * COUNT + 1, step, 0)
+    lax.fori_loop(0, 2 * COUNT + 9, step, 0)
 
     pltpu.make_async_copy(fin, fin, f_rs).wait()
 

time: 104 us -> 101 us (0.971)
  Pallas kernels: 101 us -> 98.4 us
    pallas_call x1, Pallas kernels: 96.2 us -> 93.2 us  [states_over_devices(): pl.pallas_call(state_kernel, out_shape=jax.ShapeDtypeStruct((16, 2, DH, D...]
where the time goes in v4:
time: 101 us; the launch traced here: 100 us
  Pallas kernels  98.4 us (97%)
  local copies, waits for them, and re-layouts  1.23 us (1%)
    pallas_call x1, Pallas kernels, states_over_devices(): pl.pallas_call(state_kernel, out_shape=jax.ShapeDtypeStruct((16, 2, DH, D...  93.2 us
    pallas_call x1, Pallas kernels, local_terms(): pl.pallas_call(local_kernel, out_shape=[jax.ShapeDtypeStruct(q.shape, BF1...  5.23 us

profile of v4, /device:TPU:1, one launch (start us, length us, event | category | flops | bytes accessed | tf_op | source)
XLA Modules:
  0.0 100.4 jit_solution(3633048209805350152)
XLA Ops:
  0.6 0.0 copy-start.4
  0.6 0.0 copy-start.3
  0.7 0.0 copy-start.2
  0.7 0.0 copy-start.1
  0.7 93.2 %carried_states.1.f_ref = bf16[16,2,128,128]{3,2,1,0:T(8,128)(2,1)} custom-call(bf16[128,2048]{1,0:T(8,128)(2,1)} %q_ref.1, bf16[128,2048]{1,0:T(8,128)(2,1)} %k_ref.1, bf16[128,2048]{1,0:T(8,128)(2,1)} %v_ref.1, bf16[128,2048]{1,0:T(8,128)(2,1)} %g_ref.1), custom_call_target="tpu_custom_call" | custom-call | tf_op jit(solution)/shard_map/carried_states/pallas_call | solution.py:286
  93.9 0.0 copy-done.4
  93.9 0.0 copy-done.3
  93.9 0.0 copy-done.2
  93.9 0.0 copy-done.1
  93.9 0.0 copy-start
  93.9 1.2 %copy-done = bf16[16,2,128,128]{3,2,1,0:T(8,128)(2,1)S(1)} copy-done((bf16[16,2,128,128]{3,2,1,0:T(8,128)(2,1)S(1)}, bf16[16,2,128,128]{3,2,1,0:T(8,128)(2,1)}, u32[]{:S(2)}) %copy-start) | copy-done | bytes 1048600
  95.1 5.2 %chunk_terms.1 = (bf16[128,2048]{1,0:T(8,128)(2,1)}, bf16[128,2048]{1,0:T(8,128)(2,1)}, bf16[128,2048]{1,0:T(8,128)(2,1)}, bf16[128,2048]{1,0:T(8,128)(2,1)}) custom-call(bf16[128,2048]{1,0:T(8,128)(2,1)S(1)} %copy-done.1, bf16[128,2048]{1,0:T(8,128)(2,1)S(1)} %copy-done.2, bf16[128,2048]{1,0:T(8,128)(2,1)S(1)} %copy-done.3, ...), custom_call_target="tpu_custom_call" | custom-call | tf_op jit(solution)/shard_map/chunk_terms/pallas_call | solution.py:341
Async XLA Ops:
  0.6 93.2 %copy-start.4 = (bf16[128,2048]{1,0:T(8,128)(2,1)S(1)}, bf16[128,2048]{1,0:T(8,128)(2,1)}, u32[]{:S(2)}) copy-start(bf16[128,2048]{1,0:T(8,128)(2,1)} %g_ref.1) | copy-start | bytes 1572868
  0.6 93.2 %copy-start.3 = (bf16[128,2048]{1,0:T(8,128)(2,1)S(1)}, bf16[128,2048]{1,0:T(8,128)(2,1)}, u32[]{:S(2)}) copy-start(bf16[128,2048]{1,0:T(8,128)(2,1)} %v_ref.1) | copy-start | bytes 1572868
  0.7 93.2 %copy-start.2 = (bf16[128,2048]{1,0:T(8,128)(2,1)S(1)}, bf16[128,2048]{1,0:T(8,128)(2,1)}, u32[]{:S(2)}) copy-start(bf16[128,2048]{1,0:T(8,128)(2,1)} %k_ref.1) | copy-start | bytes 1572868
  0.7 93.2 %copy-start.1 = (bf16[128,2048]{1,0:T(8,128)(2,1)S(1)}, bf16[128,2048]{1,0:T(8,128)(2,1)}, u32[]{:S(2)}) copy-start(bf16[128,2048]{1,0:T(8,128)(2,1)} %q_ref.1) | copy-start | bytes 1572868
  93.9 1.2 %copy-start = (bf16[16,2,128,128]{3,2,1,0:T(8,128)(2,1)S(1)}, bf16[16,2,128,128]{3,2,1,0:T(8,128)(2,1)}, u32[]{:S(2)}) copy-start(bf16[16,2,128,128]{3,2,1,0:T(8,128)(2,1)} %carried_states.1.f_ref) | copy-start | bytes 3145732
